TPU v7x, 512 devices: a whole 4x4x16 slice. The times are simulated.
512 devices in a mesh: rep: 128 (over x, z, core), tp: 4 (over y).
Axes of the slice: x: 4, y: 4, z: 16, core: 2. Of those that a mesh axis runs over, the one named last changes fastest.
Arguments:
- tokens: bfloat16 [16384, 1024], P('rep', 'tp'), may hold values from -6 to 6
- attn_gain: float32 [1024], replicated, may hold values from 0.1 to 1.9
- ffn_gain: float32 [1024], replicated, may hold values from 0.1 to 1.9
- w_query: bfloat16 [1024, 1024], P(None, 'tp'), may hold values from -0.0625 to 0.0625
- w_key: bfloat16 [1024, 1024], P(None, 'tp'), may hold values from -0.1875 to 0.1875
- w_value: bfloat16 [1024, 1024], P(None, 'tp'), may hold values from -0.1875 to 0.1875
- w_out: bfloat16 [1024, 1024], P('tp'), may hold values from -0.1875 to 0.1875
- w_inner: bfloat16 [1024, 2048], P(None, 'tp'), may hold values from -0.1875 to 0.1875
- w_outer: bfloat16 [2048, 1024], P('tp'), may hold values from -0.125 to 0.125
- bias_table: float32 [32, 16], P(None, 'tp'), may hold values from -3 to 3
- cache_keys: bfloat16 [256, 64, 1024], P('rep', None, 'tp'), may hold values from -68 to 68
- cache_values: bfloat16 [256, 64, 1024], P('rep', None, 'tp'), may hold values from -6 to 6
- new_counts: int32 [2, 128], P(None, 'rep'), may hold values from 1 to 64, 4096 in all within a row
- cached_lengths: int32 [2, 128], P(None, 'rep'), may hold values from 1 to 64, 4096 in all within a row
- deal: int32 [128, 128], P('rep'), may hold values from 0 to 127, each once within a row
Outputs:
- dealt: bfloat16 [16384, 1024], P('rep', 'tp')
Inputs may be any that keep to these rules, and one draw needn't show every extreme that they name: `new_counts`: for each j the counts over the replicas sum to 4096. `cached_lengths`: for each j the lengths over the replicas sum to 4096. `deal`: each row holds every number of 0 to 127 once.
All inputs are finite; a program needn't handle non-finite values. No bound on the sum of `new_counts` or of `cached_lengths` on one device may be relied on, other than what follows from the above.
Results may differ from a plain program's by a relative error of at most 0.013.
The roundings to bfloat16 on the way count: a program that leaves them out, or rounds other values in their place, can miss the bound.
Values may be sent and summed in bfloat16 or wider, within the bound.
A program may use at most 64 MiB of HBM per device.

v0:
```python
import jax
import jax.numpy as jnp
from jax import lax
from jax.sharding import PartitionSpec as P

EPSILON = 1e-06
THRESHOLDS = (12, 16, 23, 32, 46, 64, 91)


def bucket_of(relative):
    distance = jnp.abs(relative)
    larger = 8 + sum(((distance >= threshold).astype(jnp.int32) for threshold in THRESHOLDS))
    near = jnp.where(distance < 8, distance, larger)
    return near + 16 * (relative > 0).astype(jnp.int32)


def arrange(values, order, replicas):
    placed = jnp.zeros_like(values).at[order].set(values)
    return placed.reshape(values.shape[0] // replicas, replicas, values.shape[1])


def on_device(
    tokens,
    attn_gain,
    ffn_gain,
    w_query,
    w_key,
    w_value,
    w_out,
    w_inner,
    w_outer,
    bias_table,
    cache_keys,
    cache_values,
    new_counts,
    cached_lengths,
    deal,
):
    requests, cached, local_width = cache_keys.shape
    token_rows = tokens.shape[0]
    new_slots = token_rows // requests
    head_count = bias_table.shape[1]
    head_size = local_width // head_count
    replicas = lax.axis_size("rep")
    share_width = tokens.shape[1]
    first_col = lax.axis_index("tp") * share_width
    gathered = lax.all_gather(tokens, "tp", axis=1, tiled=True)
    model_width = gathered.shape[1]
    stream = gathered.astype(jnp.float32)
    inverse = lax.rsqrt(jnp.mean(stream * stream, axis=1, keepdims=True) + EPSILON)
    normed = (stream * inverse * attn_gain).astype(jnp.bfloat16)
    queries = jnp.dot(normed, w_query, preferred_element_type=jnp.float32).astype(jnp.bfloat16)
    new_keys = jnp.dot(normed, w_key, preferred_element_type=jnp.float32).astype(jnp.bfloat16)
    new_values = jnp.dot(normed, w_value, preferred_element_type=jnp.float32).astype(jnp.bfloat16)
    key_slots = cached + new_slots
    queries = queries.reshape(requests, new_slots, head_count, head_size)
    all_keys = jnp.concatenate(
        [cache_keys, new_keys.reshape(requests, new_slots, local_width)], axis=1
    ).reshape(requests, key_slots, head_count, head_size)
    all_values = jnp.concatenate(
        [cache_values, new_values.reshape(requests, new_slots, local_width)], axis=1
    ).reshape(requests, key_slots, head_count, head_size)
    counts = new_counts[:, 0]
    lengths = cached_lengths[:, 0]
    key_index = jnp.arange(key_slots, dtype=jnp.int32)
    offsets = jnp.arange(new_slots, dtype=jnp.int32)
    is_cache = key_index[None, :] < cached
    key_position = jnp.where(
        is_cache, key_index[None, :], lengths[:, None] + key_index[None, :] - cached
    )
    live_key = jnp.where(
        is_cache,
        key_index[None, :] < lengths[:, None],
        key_index[None, :] - cached < counts[:, None],
    )
    relative = key_position[:, None, :] - (lengths[:, None] + offsets[None, :])[:, :, None]
    rel_bias = jnp.take(bias_table.T, bucket_of(relative), axis=1)
    scores = jnp.einsum("gqhd,gkhd->ghqk", queries, all_keys, preferred_element_type=jnp.float32)
    scores = scores + jnp.moveaxis(rel_bias, 0, 1)
    scores = jnp.where(live_key[:, None, None, :], scores, -1e30)
    row_max = jnp.max(scores, axis=3, keepdims=True)
    weights = jnp.exp(scores - row_max)
    attn_probs = (weights / jnp.sum(weights, axis=3, keepdims=True)).astype(jnp.bfloat16)
    context = jnp.einsum(
        "ghqk,gkhd->gqhd", attn_probs, all_values, preferred_element_type=jnp.float32
    )
    context = context.astype(jnp.bfloat16).reshape(token_rows, local_width)
    partial_value = jnp.dot(context, w_out, preferred_element_type=jnp.float32)
    live_rows = (offsets[None, :] < counts[:, None]).reshape(token_rows, 1)
    order = deal[0]
    summed = lax.psum(partial_value, "tp")
    mixed = jnp.where(live_rows, stream + summed, 0.0)
    dealt_rows = lax.all_to_all(
        arrange(mixed, order, replicas), "rep", split_axis=1, concat_axis=0, tiled=True
    ).reshape(token_rows, model_width)
    inverse_ffn = lax.rsqrt(jnp.mean(dealt_rows * dealt_rows, axis=1, keepdims=True) + EPSILON)
    ffn_input = (dealt_rows * inverse_ffn * ffn_gain).astype(jnp.bfloat16)
    own_cols = lax.dynamic_slice_in_dim(dealt_rows, first_col, share_width, 1)
    hidden = jnp.maximum(
        jnp.dot(ffn_input, w_inner, preferred_element_type=jnp.float32), 0.0
    ).astype(jnp.bfloat16)
    projected = jnp.dot(hidden, w_outer, preferred_element_type=jnp.float32)
    ffn_share = lax.psum_scatter(
        projected.astype(jnp.bfloat16), "tp", scatter_dimension=1, tiled=True
    ).astype(jnp.float32)
    return (own_cols + ffn_share).astype(jnp.bfloat16)


def solution(mesh):
    in_specs = (
        P("rep", "tp"),
        P(),
        P(),
        P(None, "tp"),
        P(None, "tp"),
        P(None, "tp"),
        P("tp", None),
        P(None, "tp"),
        P("tp", None),
        P(None, "tp"),
        P("rep", None, "tp"),
        P("rep", None, "tp"),
        P(None, "rep"),
        P(None, "rep"),
        P("rep", None),
    )
    out_specs = P("rep", "tp")
    return jax.shard_map(
        on_device, mesh=mesh, in_specs=in_specs, out_specs=out_specs, check_vma=False
    )
```

profile of v0, /device:TPU:1, one launch (start us, length us, event | category | flops | bytes accessed | tf_op | source)
XLA Modules:
  0.0 233.6 jit_solution(14345689642825715247)
XLA Ops:
  6.5 0.0 copy-start
  6.5 0.0 copy-start.5
  6.5 0.0 copy-start.7
  6.5 0.0 copy-start.2
  6.5 0.0 copy-start.6
  6.5 0.0 all-reduce.2.cloned.1.call-start
  6.6 0.8 iota_add_fusion
  7.4 0.7 add_select_fusion
  8.1 0.1 compare_select_fusion
  8.3 0.2 compare_and_fusion
  8.5 10.9 %all_gather.3 = bf16[128,1024]{1,0:T(8,128)(2,1)S(1)} all-gather(bf16[128,256]{1,0:T(8,128)(2,1)} %param.15), channel_id=1, replica_groups=mesh['rep'=128,'tp'=4] {'tp'}, dimensions={1}, use_global_device_ids=true | all-gather | bytes 327680 | tf_op jit(solution)/shard_map/all_gather | solution.py:47
  19.4 0.0 copy-start.3
  19.4 0.1 fusion.6
  19.5 1.3 convolution_convert_fusion.2
  20.9 0.1 concatenate.20
  21.0 0.1 copy.34
  21.1 1.3 convolution_convert_fusion.3
  22.5 0.1 reshape.311
  22.6 0.8 copy.36
  23.4 0.0 copy-start.8
  23.4 54.4 %gather_fusion = f32[16384,4]{1,0:T(8,128)} fusion(f32[4,32]{0,1:T(8,128)S(1)} %bitcast.40, s32[16384]{0:T(1024)S(1)} %broadcast_clamp_fusion), kind=kCustom, calls=%fused_computation | custom fusion | bytes 589824 | tf_op jit(solution)/shard_map/jit(_take)/gather | solution.py:77
  77.8 0.0 copy-start.1
  77.8 0.0 copy-start.4
  77.8 5.3 %copy.38 = f32[2,64,128,4]{2,1,3,0:T(8,128)S(1)} copy(f32[2,64,128,4]{3,2,1,0:T(8,128)} %bitcast.41) | data formatting | bytes 524288 | tf_op jit(solution)/shard_map/jit(_take)/gather | solution.py:77
  83.1 0.0 copy-done.2
  83.1 0.1 copy.33
  83.3 0.0 copy-done.5
  83.3 0.0 copy-done.6
  83.3 0.1 compare_select_fusion.5
  83.4 0.2 fusion.2
  83.6 0.2 fusion.57
  83.9 0.0 copy-done.7
  83.9 1.3 convolution_convert_fusion.4
  85.2 0.1 concatenate.17
  85.3 0.1 copy.32
  85.5 0.0 copy-done.3
  85.5 0.1 copy.31
  85.6 1.0 fusion.5
  86.7 0.1 copy.39
  86.8 0.1 reshape.312
  87.0 2.1 fusion.58
  89.0 0.0 all-reduce.2.cloned.1.call-update
  89.1 0.0 reduce-scatter.2.cloned.1.call-start
  89.1 0.1 iota_compare_fusion
  89.2 0.1 lt.127
  89.3 0.0 copy-done.8
  89.3 62.9 %all-reduce.2.cloned.1.call-done = f32[128,1024]{1,0:T(8,128)} async-done(((f32[128,1024]{1,0:T(8,128)}), f32[128,1024]{1,0:T(8,128)}) %all-reduce.2.cloned.1.call-update) | async-done | bytes 524304 | tf_op jit(solution)/shard_map/psum | solution.py:91
  152.2 1.7 scatter_custom_fusion
  154.0 0.5 copy.40
  154.5 51.8 %all_to_all.4 = f32[1,128,1024]{2,0,1:T(1,128)S(1)} all-to-all(f32[1,128,1024]{2,0,1:T(1,128)S(1)} %copy.40), channel_id=1, replica_groups=mesh['rep'=128,'tp'=4] {'rep'}, dimensions={1} | all-to-all | bytes 1048576 | tf_op jit(solution)/shard_map/all_to_all | solution.py:93
  206.3 0.2 fusion.10
  206.4 0.0 copy-done
  206.4 0.0 copy-done.1
  206.5 0.0 copy-done.4
  206.5 1.3 convolution_convert_fusion
  207.8 0.0 reduce-scatter.2.cloned.1.call-update
  207.8 0.1 constant_dynamic-slice_fusion
  207.9 17.4 %reduce-scatter.2.cloned.1.call-done = bf16[128,256]{1,0:T(8,128)(2,1)} async-done(((bf16[128,1024]{1,0:T(8,128)(2,1)}), bf16[128,256]{1,0:T(8,128)(2,1)}) %reduce-scatter.2.cloned.1.call-update) | async-done | bytes 65552 | tf_op jit(solution)/shard_map/reduce_scatter | solution.py:103
  225.2 1.5 fusion.29
  (6 shorter events, 0.0 us)
Async XLA Ops:
  6.5 199.9 %copy-start = (bf16[512,1024]{1,0:T(8,128)(2,1)S(1)}, bf16[512,1024]{1,0:T(8,128)(2,1)}, u32[]{:S(2)}) copy-start(bf16[512,1024]{1,0:T(8,128)(2,1)} %param.23) | copy-start | bytes 3145732
  6.5 76.7 %copy-start.5 = (s32[2,1]{0,1:T(1,128)S(1)}, s32[2,1]{0,1:T(1,128)}, u32[]{:S(2)}) copy-start(s32[2,1]{0,1:T(1,128)} %param.28) | copy-start | bytes 28
  6.5 77.3 %copy-start.7 = (f32[1024]{0:T(1024)S(1)}, f32[1024]{0:T(1024)}, u32[]{:S(2)}) copy-start(f32[1024]{0:T(1024)} %param.16) | copy-start | bytes 12292
  6.5 76.6 %copy-start.2 = (bf16[2,64,256]{2,1,0:T(8,128)(2,1)S(1)}, bf16[2,64,256]{2,1,0:T(8,128)(2,1)}, u32[]{:S(2)}) copy-start(bf16[2,64,256]{2,1,0:T(8,128)(2,1)} %param.25) | copy-start | bytes 196612
  6.5 76.7 %copy-start.6 = (s32[2,1]{0,1:T(1,128)S(1)}, s32[2,1]{0,1:T(1,128)}, u32[]{:S(2)}) copy-start(s32[2,1]{0,1:T(1,128)} %param.27) | copy-start | bytes 28
  6.5 145.7 %all-reduce.2.cloned.1.call-start = ((), (), s32[]{:S(2)}) async-start(), calls=%async_computation.2 | async-start | bytes 1048576 | tf_op jit(solution)/shard_map/psum | solution.py:91
  19.4 66.1 %copy-start.3 = (bf16[2,64,256]{2,1,0:T(8,128)(2,1)S(1)}, bf16[2,64,256]{2,1,0:T(8,128)(2,1)}, u32[]{:S(2)}) copy-start(bf16[2,64,256]{2,1,0:T(8,128)(2,1)} %param.26) | copy-start | bytes 196612
  23.4 65.9 %copy-start.8 = (s32[1,128]{1,0:T(1,128)S(1)}, s32[1,128]{1,0:T(1,128)}, u32[]{:S(2)}) copy-start(s32[1,128]{1,0:T(1,128)} %param.29) | copy-start | bytes 1540
  77.8 128.6 %copy-start.1 = (bf16[1024,512]{1,0:T(8,128)(2,1)S(1)}, bf16[1024,512]{1,0:T(8,128)(2,1)}, u32[]{:S(2)}) copy-start(bf16[1024,512]{1,0:T(8,128)(2,1)} %param.22) | copy-start | bytes 3145732
  77.8 128.6 %copy-start.4 = (f32[1024]{0:T(1024)S(1)}, f32[1024]{0:T(1024)}, u32[]{:S(2)}) copy-start(f32[1024]{0:T(1024)} %param.17) | copy-start | bytes 12292
  89.1 136.2 %reduce-scatter.2.cloned.1.call-start = ((), (), s32[]{:S(2)}) async-start(), calls=%async_computation.3 | async-start | bytes 327680 | tf_op jit(solution)/shard_map/reduce_scatter | solution.py:103
Sparse Core Ops, SparseCore 0:
  89.2 62.9 all-reduce.1
  207.9 17.2 reduce-scatter.1
where the time goes:
time: 235 us; the launch traced here: 234 us
  waiting for transfers between devices  80.4 us (34%)
  blocking collectives  62.7 us (27%)
  local copies, waits for them, and re-layouts  62.4 us (27%)
  between operations  13.6 us (6%)
  matrix products  8.65 us (4%)
  other arithmetic  5.78 us (2%)
    psum x1, waiting for transfers between devices, on_device(): summed = lax.psum(partial_value, 'tp')  62.9 us
    gather x2, local copies, waits for them, and re-layouts, on_device(): rel_bias = jnp.take(bias_table.T, bucket_of(relative), axis=1)  59.7 us
    all_to_all x1, blocking collectives, on_device(): lax.all_to_all(arrange(mixed, order, replicas), 'rep', split_axis=1, conc...  51.8 us
    reduce_scatter x1, waiting for transfers between devices, on_device(): lax.psum_scatter(projected.astype(jnp.bfloat16), 'tp', scatter_dimension=...  17.4 us
    all_gather x1, blocking collectives, on_device(): gathered = lax.all_gather(tokens, 'tp', axis=1, tiled=True)  10.9 us
  transfers between devices with their start and end apart: 2, of which 2 were waited for; matrix products, arithmetic and copies ran while one was open for 0% of the time, Pallas kernels for 0%

commit v1 on v0

v1 whole, which is shorter than its diff:
```python
import jax
import jax.numpy as jnp
from jax import lax
from jax.experimental import pallas as pl
from jax.experimental.pallas import tpu as pltpu
from jax.sharding import PartitionSpec as P

EPSILON = 1e-06
THRESHOLDS = (12, 16, 23, 32, 46, 64, 91)
BUCKETS = 32
TP = 4
SIDES = 8
DEPTH = 16
MESH = pl.DeviceIdType.MESH
BF16 = jnp.bfloat16
F32 = jnp.float32


def iota(shape, dim):
    return lax.broadcasted_iota(jnp.int32, shape, dim)


def dot(a, b):
    return jnp.dot(a, b, preferred_element_type=F32)


def dot_t(a, b):
    return lax.dot_general(a, b, (((1,), (1,)), ((), ())), preferred_element_type=F32)


def bucket_of(relative):
    distance = jnp.abs(relative)
    larger = 8 + sum(((distance >= threshold).astype(jnp.int32) for threshold in THRESHOLDS))
    near = jnp.where(distance < 8, distance, larger)
    return near + 16 * (relative > 0).astype(jnp.int32)


def one_hot(condition):
    return jnp.where(condition, 1.0, 0.0).astype(BF16)


def kernel(
    tokens_ref,
    attn_gain_ref,
    ffn_gain_ref,
    w_query_ref,
    w_key_ref,
    w_value_ref,
    w_out_ref,
    w_inner_ref,
    w_outer_ref,
    bias_ref,
    cache_k_ref,
    cache_v_ref,
    counts_ref,
    lengths_ref,
    deal_ref,
    out_ref,
    x_full,
    w_qkv,
    w_out,
    w_inner,
    w_outer,
    cache_k,
    cache_v,
    bias,
    partial,
    send_rows,
    recv_rows,
    ffn_full,
    send_cols,
    recv_cols,
    side_send,
    side_recv,
    z_send,
    z_recv,
    load_sem,
    ag_send,
    ag_recv,
    rs_send,
    rs_recv,
    ag2_send,
    ag2_recv,
    rs2_send,
    rs2_recv,
    side_send_sem,
    side_recv_sem,
    z_send_sem,
    z_recv_sem,
):
    rep = lax.axis_index("rep")
    tp = lax.axis_index("tp")
    tokens, width = tokens_ref.shape
    model = w_qkv.shape[0]
    requests, cached, _ = cache_k_ref.shape
    slots = tokens // requests
    heads = bias_ref.shape[1]
    hdim = width // heads
    keys = cached + slots
    own = tokens // TP
    x_at, z_at, core = rep // (2 * DEPTH), (rep // 2) % DEPTH, rep % 2
    side = x_at * 2 + core

    def tp_peer(offset):
        return (tp + offset) % TP

    def side_peer(offset):
        other = (side + offset) % SIDES
        return other, (other // 2) * (2 * DEPTH) + z_at * 2 + other % 2

    def z_peer(offset):
        other = (z_at + offset) % DEPTH
        return other, x_at * (2 * DEPTH) + other * 2 + core

    barrier = pltpu.get_barrier_semaphore()
    for offset in range(1, TP):
        pl.semaphore_signal(barrier, inc=1, device_id={"tp": tp_peer(offset)}, device_id_type=MESH)
    for offset in range(1, SIDES):
        pl.semaphore_signal(barrier, inc=1, device_id={"rep": side_peer(offset)[1]}, device_id_type=MESH)
    for offset in range(1, DEPTH):
        pl.semaphore_signal(barrier, inc=1, device_id={"rep": z_peer(offset)[1]}, device_id_type=MESH)

    own_cols = pl.ds(pl.multiple_of(tp * width, width), width)
    own_rows = pl.ds(pl.multiple_of(tp * own, own), own)

    loads = [
        pltpu.make_async_copy(src, dst, load_sem.at[i])
        for i, (src, dst) in enumerate(
            [
                (tokens_ref, x_full.at[:, own_cols]),
                (w_query_ref, w_qkv.at[:, pl.ds(0, width)]),
                (w_key_ref, w_qkv.at[:, pl.ds(width, width)]),
                (w_value_ref, w_qkv.at[:, pl.ds(2 * width, width)]),
                (cache_k_ref, cache_k),
                (cache_v_ref, cache_v),
                (w_out_ref, w_out),
                (w_inner_ref, w_inner),
                (w_outer_ref, w_outer),
            ]
        )
    ]
    for load in loads:
        load.start()

    pl.semaphore_wait(barrier, (TP - 1) + (SIDES - 1) + (DEPTH - 1))

    loads[0].wait()
    gathers = []
    for offset in (2, 1, 3):
        copy = pltpu.make_async_remote_copy(
            src_ref=x_full.at[:, own_cols],
            dst_ref=x_full.at[:, own_cols],
            send_sem=ag_send.at[offset - 1],
            recv_sem=ag_recv.at[offset - 1],
            device_id={"tp": tp_peer(offset)},
            device_id_type=MESH,
        )
        copy.start()
        gathers.append(copy)

    key = iota((slots, keys), 1)
    query = iota((slots, keys), 0)
    for r in range(requests):
        length = lengths_ref[r, 0]
        position = jnp.where(key < cached, key, length + key - cached)
        bucket = bucket_of(position - (length + query))
        rows = [jnp.zeros((slots, keys), F32) for _ in range(heads)]
        for b in range(BUCKETS):
            here = bucket == b
            rows = [jnp.where(here, bias_ref[b, h], rows[h]) for h in range(heads)]
        for h in range(heads):
            bias[r, pl.ds(h * slots, slots), :] = rows[h]

    q_row = iota((tokens, tokens), 0)
    k_col = iota((tokens, tokens), 1)
    q_side, q_z = q_row // DEPTH, q_row % DEPTH
    destination = (q_side // 2) * (2 * DEPTH) + q_z * 2 + q_side % 2
    count_of = jnp.where(k_col // slots == 0, counts_ref[0, 0], counts_ref[requests - 1, 0])
    live = (k_col % slots) < count_of
    order = jnp.where((deal_ref[...] == destination) & live, 1.0, 0.0)

    for copy in gathers:
        copy.wait_recv()

    stream = x_full[...].astype(F32)
    inverse = lax.rsqrt(jnp.mean(stream * stream, axis=1, keepdims=True) + EPSILON)
    normed = (stream * inverse * attn_gain_ref[...]).astype(BF16)
    for load in loads[1:4]:
        load.wait()
    qkv = dot(normed, w_qkv[...]).astype(BF16)

    loads[4].wait()
    loads[5].wait()
    lane_head = iota((slots, width), 1) // hdim
    key_row = iota((heads * slots, keys), 1)
    contexts = []
    for r in range(requests):
        rows = slice(r * slots, (r + 1) * slots)
        queries = qkv[rows, 0:width]
        all_keys = jnp.concatenate([cache_k[r], qkv[rows, width : 2 * width]], axis=0)
        all_values = jnp.concatenate([cache_v[r], qkv[rows, 2 * width :]], axis=0)
        stacked = jnp.concatenate(
            [jnp.where(lane_head == h, queries, jnp.zeros_like(queries)) for h in range(heads)], axis=0
        )
        scores = dot_t(stacked, all_keys) + bias[r]
        limit = jnp.where(key_row < cached, lengths_ref[r, 0], cached + counts_ref[r, 0])
        scores = jnp.where(key_row < limit, scores, -1e30)
        weights = jnp.exp(scores - jnp.max(scores, axis=1, keepdims=True))
        probs = (weights / jnp.sum(weights, axis=1, keepdims=True)).astype(BF16)
        spread = dot(probs, all_values)
        context = jnp.zeros((slots, width), F32)
        for h in range(heads):
            context = jnp.where(lane_head == h, spread[h * slots : (h + 1) * slots], context)
        contexts.append(context.astype(BF16))
    context = jnp.concatenate(contexts, axis=0)

    moved = dot(order.astype(BF16), context).astype(BF16)
    loads[6].wait()
    partial[...] = dot(moved, w_out[...])
    send_rows[...] = partial[...].astype(BF16)
    row_sends = []
    for offset in (2, 1, 3):
        peer = tp_peer(offset)
        copy = pltpu.make_async_remote_copy(
            src_ref=send_rows.at[pl.ds(pl.multiple_of(peer * own, own), own), :],
            dst_ref=recv_rows.at[offset - 1],
            send_sem=rs_send.at[offset - 1],
            recv_sem=rs_recv.at[offset - 1],
            device_id={"tp": peer},
            device_id_type=MESH,
        )
        copy.start()
        row_sends.append(copy)

    own_q = iota((own, tokens), 0) + tp * own
    own_k = iota((own, tokens), 1)
    own_side, own_z = own_q // DEPTH, own_q % DEPTH
    own_destination = (own_side // 2) * (2 * DEPTH) + own_z * 2 + own_side % 2
    own_count = jnp.where(own_k // slots == 0, counts_ref[0, 0], counts_ref[requests - 1, 0])
    own_order = one_hot((deal_ref[...] == own_destination) & ((own_k % slots) < own_count))
    mixed = dot(own_order, x_full[...]) + partial[own_rows, :]

    for copy in row_sends:
        copy.wait_recv()
    mixed = mixed + (recv_rows[0].astype(F32) + recv_rows[1].astype(F32) + recv_rows[2].astype(F32))
    inverse_ffn = lax.rsqrt(jnp.mean(mixed * mixed, axis=1, keepdims=True) + EPSILON)
    ffn_full[own_rows, :] = (mixed * inverse_ffn * ffn_gain_ref[...]).astype(BF16)
    ffn_gathers = []
    for offset in (2, 1, 3):
        copy = pltpu.make_async_remote_copy(
            src_ref=ffn_full.at[own_rows, :],
            dst_ref=ffn_full.at[own_rows, :],
            send_sem=ag2_send.at[offset - 1],
            recv_sem=ag2_recv.at[offset - 1],
            device_id={"tp": tp_peer(offset)},
            device_id_type=MESH,
        )
        copy.start()
        ffn_gathers.append(copy)
    loads[7].wait()
    loads[8].wait()
    for copy in ffn_gathers:
        copy.wait_recv()

    hidden = jnp.maximum(dot(ffn_full[...], w_inner[...]), 0.0).astype(BF16)
    partial[...] = dot(hidden, w_outer[...])
    partial[own_rows, :] = partial[own_rows, :] + mixed
    send_cols[...] = partial[...].astype(BF16)
    col_sends = []
    for offset in (2, 1, 3):
        peer = tp_peer(offset)
        copy = pltpu.make_async_remote_copy(
            src_ref=send_cols.at[:, pl.ds(pl.multiple_of(peer * width, width), width)],
            dst_ref=recv_cols.at[offset - 1],
            send_sem=rs2_send.at[offset - 1],
            recv_sem=rs2_recv.at[offset - 1],
            device_id={"tp": peer},
            device_id_type=MESH,
        )
        copy.start()
        col_sends.append(copy)
    to_row = iota((2 * tokens, 2 * tokens), 0)
    to_col = iota((2 * tokens, 2 * tokens), 1)
    gather_z = one_hot(
        to_col
        == ((to_row // SIDES) % 2) * tokens + (to_row % SIDES) * DEPTH + to_row // (2 * SIDES)
    )
    final = partial[:, own_cols]
    for copy in col_sends:
        copy.wait_recv()
    final = final + (recv_cols[0].astype(F32) + recv_cols[1].astype(F32) + recv_cols[2].astype(F32))
    side_send[...] = final.astype(BF16).reshape(SIDES, DEPTH, width)

    side_sends = []
    for offset in range(1, SIDES):
        other, peer = side_peer(offset)
        copy = pltpu.make_async_remote_copy(
            src_ref=side_send.at[other],
            dst_ref=side_recv.at[side],
            send_sem=side_send_sem.at[offset - 1],
            recv_sem=side_recv_sem.at[offset - 1],
            device_id={"rep": peer},
            device_id_type=MESH,
        )
        copy.start()
        side_sends.append(copy)
    side_recv[side] = side_send[side]
    d_row = iota((tokens, 2 * tokens), 0)
    d_col = iota((tokens, 2 * tokens), 1)
    d_from = ((d_row // 2) % DEPTH) * (2 * SIDES) + (d_row // (2 * DEPTH)) * 2 + d_row % 2
    left = one_hot(d_col == d_from)
    right = one_hot(d_col == d_from + SIDES)
    for copy in side_sends:
        copy.wait_recv()

    arrived = side_recv[...].reshape(tokens, width)
    halves = jnp.concatenate([arrived[:, : width // 2], arrived[:, width // 2 :]], axis=0)
    z_send[...] = dot(gather_z, halves).astype(BF16).reshape(DEPTH, 2 * SIDES, width // 2)
    z_sends = []
    for offset in range(1, DEPTH):
        other, peer = z_peer(offset)
        copy = pltpu.make_async_remote_copy(
            src_ref=z_send.at[other],
            dst_ref=z_recv.at[z_at],
            send_sem=z_send_sem.at[offset - 1],
            recv_sem=z_recv_sem.at[offset - 1],
            device_id={"rep": peer},
            device_id_type=MESH,
        )
        copy.start()
        z_sends.append(copy)
    z_recv[z_at] = z_send[z_at]
    for copy in gathers + row_sends + ffn_gathers + col_sends + side_sends:
        copy.wait_send()
    for copy in z_sends:
        copy.wait_recv()
    landed = z_recv[...].reshape(2 * tokens, width // 2)
    out_ref[:, : width // 2] = dot(left, landed).astype(BF16)
    out_ref[:, width // 2 :] = dot(right, landed).astype(BF16)
    for copy in z_sends:
        copy.wait_send()


def on_device(
    tokens,
    attn_gain,
    ffn_gain,
    w_query,
    w_key,
    w_value,
    w_out,
    w_inner,
    w_outer,
    bias_table,
    cache_keys,
    cache_values,
    new_counts,
    cached_lengths,
    deal,
):
    rows, width = tokens.shape
    model = w_query.shape[0]
    ff = w_inner.shape[1]
    requests, cached, _ = cache_keys.shape
    slots = rows // requests
    heads = bias_table.shape[1]
    own = rows // TP
    hbm = pl.BlockSpec(memory_space=pltpu.HBM)
    vmem = pl.BlockSpec(memory_space=pltpu.VMEM)
    smem = pl.BlockSpec(memory_space=pltpu.SMEM)
    dma = pltpu.SemaphoreType.DMA
    return pl.pallas_call(
        kernel,
        out_shape=jax.ShapeDtypeStruct((rows, width), BF16),
        in_specs=[
            hbm, vmem, vmem, hbm, hbm, hbm, hbm, hbm, hbm, smem, hbm, hbm, smem, smem, vmem,
        ],
        out_specs=vmem,
        scratch_shapes=[
            pltpu.VMEM((rows, model), BF16),
            pltpu.VMEM((model, 3 * width), BF16),
            pltpu.VMEM((width, model), BF16),
            pltpu.VMEM((model, ff), BF16),
            pltpu.VMEM((ff, model), BF16),
            pltpu.VMEM((requests, cached, width), BF16),
            pltpu.VMEM((requests, cached, width), BF16),
            pltpu.VMEM((requests, heads * slots, cached + slots), F32),
            pltpu.VMEM((rows, model), F32),
            pltpu.VMEM((rows, model), BF16),
            pltpu.VMEM((TP - 1, own, model), BF16),
            pltpu.VMEM((rows, model), BF16),
            pltpu.VMEM((rows, model), BF16),
            pltpu.VMEM((TP - 1, rows, width), BF16),
            pltpu.VMEM((SIDES, DEPTH, width), BF16),
            pltpu.VMEM((SIDES, DEPTH, width), BF16),
            pltpu.VMEM((DEPTH, 2 * SIDES, width // 2), BF16),
            pltpu.VMEM((DEPTH, 2 * SIDES, width // 2), BF16),
            dma((9,)),
            dma((TP - 1,)),
            dma((TP - 1,)),
            dma((TP - 1,)),
            dma((TP - 1,)),
            dma((TP - 1,)),
            dma((TP - 1,)),
            dma((TP - 1,)),
            dma((TP - 1,)),
            dma((SIDES - 1,)),
            dma((SIDES - 1,)),
            dma((DEPTH - 1,)),
            dma((DEPTH - 1,)),
        ],
        compiler_params=pltpu.CompilerParams(
            collective_id=0, has_side_effects=True, vmem_limit_bytes=40 * 1024 * 1024
        ),
    )(
        tokens,
        attn_gain.reshape(1, model),
        ffn_gain.reshape(1, model),
        w_query,
        w_key,
        w_value,
        w_out,
        w_inner,
        w_outer,
        bias_table,
        cache_keys,
        cache_values,
        new_counts,
        cached_lengths,
        deal,
    )


def solution(mesh):
    in_specs = (
        P("rep", "tp"),
        P(),
        P(),
        P(None, "tp"),
        P(None, "tp"),
        P(None, "tp"),
        P("tp", None),
        P(None, "tp"),
        P("tp", None),
        P(None, "tp"),
        P("rep", None, "tp"),
        P("rep", None, "tp"),
        P(None, "rep"),
        P(None, "rep"),
        P("rep", None),
    )
    out_specs = P("rep", "tp")
    return jax.shard_map(
        on_device, mesh=mesh, in_specs=in_specs, out_specs=out_specs, check_vma=False
    )
```

time: 235 us -> 62 us (0.26)
  waiting for transfers between devices: 80.4 us -> 0 us
  blocking collectives: 62.7 us -> 0 us
  local copies, waits for them, and re-layouts: 62.4 us -> 11.8 us
  Pallas kernels: 0 us -> 49.4 us
  between operations: 13.6 us -> 0.03 us
  matrix products: 8.65 us -> 0 us
  other arithmetic: 5.78 us -> 0 us
    psum x1 -> x0, waiting for transfers between devices: 62.9 us -> none  [on_device(): summed = lax.psum(partial_value, 'tp')]
    gather x2 -> x0, local copies, waits for them, and re-layouts: 59.7 us -> none  [on_device(): rel_bias = jnp.take(bias_table.T, bucket_of(relative), axis=1)]
    all_to_all x1 -> x0, blocking collectives: 51.8 us -> none  [on_device(): lax.all_to_all(arrange(mixed, order, replicas), 'rep', split_axis=1, conc...]
    pallas_call x0 -> x1, Pallas kernels: none -> 49.4 us  [on_device(): pl.pallas_call(kernel, out_shape=jax.ShapeDtypeStruct((rows, width), BF16...]
    reduce_scatter x1 -> x0, waiting for transfers between devices: 17.4 us -> none  [on_device(): lax.psum_scatter(projected.astype(jnp.bfloat16), 'tp', scatter_dimension=...]
    all_gather x1 -> x0, blocking collectives: 10.9 us -> none  [on_device(): gathered = lax.all_gather(tokens, 'tp', axis=1, tiled=True)]
    unnamed x21 -> x34, local copies, waits for them, and re-layouts: 1.04 us -> 11.8 us
    dot_general x7 -> x0, matrix products: 8.65 us -> none  [the longest x1 2.09 us: on_device(): partial_value = jnp.dot(context, w_out, preferred_element_type=jnp.float32)]
  transfers between devices with their start and end apart: 2 -> 0, of which waited for: 2 -> 0; matrix products, arithmetic and copies ran while one was open for 0% -> 0% of each run, Pallas kernels for 0% -> 0%
where the time goes in v1:
time: 62 us; the launch traced here: 61.3 us
  Pallas kernels  49.4 us (80%)
  local copies, waits for them, and re-layouts  11.8 us (19%)
    pallas_call x1, Pallas kernels, on_device(): pl.pallas_call(kernel, out_shape=jax.ShapeDtypeStruct((rows, width), BF16...  49.4 us
    unnamed x34, local copies, waits for them, and re-layouts  11.8 us

profile of v1, /device:TPU:1, one launch (start us, length us, event | category | flops | bytes accessed | tf_op | source)
XLA Modules:
  0.0 61.3 jit_solution(2378690996487318934)
XLA Ops:
  0.0 0.0 copy-start.13
  0.0 0.0 copy-start.14
  0.0 0.7 %copy-done.13 = s32[2,1]{0,1:T(1,128)S(1)} copy-done((s32[2,1]{0,1:T(1,128)S(1)}, s32[2,1]{0,1:T(1,128)}, u32[]{:S(2)}) %copy-start.13) | copy-done | bytes 32
  0.7 0.0 copy-start.12
  0.7 0.1 copy.17.counts_ref
  0.8 0.0 copy-done.14
  0.8 0.1 copy.18.lengths_ref
  0.8 0.5 copy-done.12
  1.3 0.0 copy-start.9
  1.3 0.0 copy-start.10
  1.3 0.0 copy-start.11
  1.3 0.1 copy.16.bias_ref
  1.4 0.6 copy-done.9
  2.0 0.0 copy-done.10
  2.0 0.0 copy-done.11
  2.0 0.0 copy-start
  2.0 1.2 %copy-done = bf16[1024,512]{1,0:T(8,128)(2,1)S(1)} copy-done((bf16[1024,512]{1,0:T(8,128)(2,1)S(1)}, bf16[1024,512]{1,0:T(8,128)(2,1)}, u32[]{:S(2)}) %copy-start) | copy-done | bytes 1048600
  3.3 0.0 copy-start.1
  3.3 1.2 %copy-done.1 = bf16[512,1024]{1,0:T(8,128)(2,1)S(1)} copy-done((bf16[512,1024]{1,0:T(8,128)(2,1)S(1)}, bf16[512,1024]{1,0:T(8,128)(2,1)}, u32[]{:S(2)}) %copy-start.1) | copy-done | bytes 1048600
  4.5 0.0 copy-start.2
  4.5 1.0 %copy-done.2 = bf16[1024,256]{1,0:T(8,128)(2,1)S(1)} copy-done((bf16[1024,256]{1,0:T(8,128)(2,1)S(1)}, bf16[1024,256]{1,0:T(8,128)(2,1)}, u32[]{:S(2)}) %copy-start.2) | copy-done | bytes 524312
  5.5 0.0 copy-start.3
  5.5 1.0 %copy-done.3 = bf16[1024,256]{1,0:T(8,128)(2,1)S(1)} copy-done((bf16[1024,256]{1,0:T(8,128)(2,1)S(1)}, bf16[1024,256]{1,0:T(8,128)(2,1)}, u32[]{:S(2)}) %copy-start.3) | copy-done | bytes 524312
  6.6 0.0 copy-start.4
  6.6 1.0 %copy-done.4 = bf16[1024,256]{1,0:T(8,128)(2,1)S(1)} copy-done((bf16[1024,256]{1,0:T(8,128)(2,1)S(1)}, bf16[1024,256]{1,0:T(8,128)(2,1)}, u32[]{:S(2)}) %copy-start.4) | copy-done | bytes 524312
  7.6 0.0 copy-start.5
  7.6 1.0 %copy-done.5 = bf16[256,1024]{1,0:T(8,128)(2,1)S(1)} copy-done((bf16[256,1024]{1,0:T(8,128)(2,1)S(1)}, bf16[256,1024]{1,0:T(8,128)(2,1)}, u32[]{:S(2)}) %copy-start.5) | copy-done | bytes 524312
  8.7 0.0 copy-start.6
  8.7 0.8 %copy-done.6 = bf16[128,256]{1,0:T(8,128)(2,1)S(1)} copy-done((bf16[128,256]{1,0:T(8,128)(2,1)S(1)}, bf16[128,256]{1,0:T(8,128)(2,1)}, u32[]{:S(2)}) %copy-start.6) | copy-done | bytes 65560
  9.5 0.0 copy-start.7
  9.5 0.8 %copy-done.7 = bf16[2,64,256]{2,1,0:T(8,128)(2,1)S(1)} copy-done((bf16[2,64,256]{2,1,0:T(8,128)(2,1)S(1)}, bf16[2,64,256]{2,1,0:T(8,128)(2,1)}, u32[]{:S(2)}) %copy-start.7) | copy-done | bytes 65560
  10.3 0.0 copy-start.8
  10.3 0.8 %copy-done.8 = bf16[2,64,256]{2,1,0:T(8,128)(2,1)S(1)} copy-done((bf16[2,64,256]{2,1,0:T(8,128)(2,1)S(1)}, bf16[2,64,256]{2,1,0:T(8,128)(2,1)}, u32[]{:S(2)}) %copy-start.8) | copy-done | bytes 65560
  11.2 49.4 %shard_map.145 = bf16[128,256]{1,0:T(8,128)(2,1)S(1)} custom-call(bf16[128,256]{1,0:T(8,128)(2,1)S(1)} %copy-done.6, f32[1,1024]{1,0:T(1,128)S(1)} %bitcast.2, f32[1,1024]{1,0:T(1,128)S(1)} %bitcast.3, bf16[1024,256]{1,0:T(8,128)(2,1)S(1)} %copy-done.2, bf16[1024,256]{1,0:T(8,128)(2,1)S(1)} %copy-done.3, bf16[1024,256]{1,0:T(8,128)(2,1)S(1)} %copy-done.4, ...), custom_call_target="tpu_custom_call" | custom-call | tf_op jit(solution)/shard_map/pallas_call | solution.py:372
  60.6 0.6 %copy.20 = bf16[128,256]{1,0:T(8,128)(2,1)} copy(bf16[128,256]{1,0:T(8,128)(2,1)S(1)} %shard_map.145) | data formatting | bytes 131072
Async XLA Ops:
  0.0 0.7 %copy-start.13 = (s32[2,1]{0,1:T(1,128)S(1)}, s32[2,1]{0,1:T(1,128)}, u32[]{:S(2)}) copy-start(s32[2,1]{0,1:T(1,128)} %param.27) | copy-start | bytes 28
  0.0 0.8 %copy-start.14 = (s32[2,1]{0,1:T(1,128)S(1)}, s32[2,1]{0,1:T(1,128)}, u32[]{:S(2)}) copy-start(s32[2,1]{0,1:T(1,128)} %param.28) | copy-start | bytes 28
  0.7 0.7 %copy-start.12 = (f32[32,4]{0,1:T(4,128)S(1)}, f32[32,4]{0,1:T(4,128)}, u32[]{:S(2)}) copy-start(f32[32,4]{0,1:T(4,128)} %param.24) | copy-start | bytes 1540
  1.3 0.7 %copy-start.9 = (f32[1024]{0:T(1024)S(1)}, f32[1024]{0:T(1024)}, u32[]{:S(2)}) copy-start(f32[1024]{0:T(1024)} %param.16) | copy-start | bytes 12292
  1.3 0.7 %copy-start.10 = (f32[1024]{0:T(1024)S(1)}, f32[1024]{0:T(1024)}, u32[]{:S(2)}) copy-start(f32[1024]{0:T(1024)} %param.17) | copy-start | bytes 12292
  1.3 0.7 %copy-start.11 = (s32[1,128]{1,0:T(1,128)S(1)}, s32[1,128]{1,0:T(1,128)}, u32[]{:S(2)}) copy-start(s32[1,128]{1,0:T(1,128)} %deal_ref.1) | copy-start | bytes 1540
  2.0 1.2 %copy-start = (bf16[1024,512]{1,0:T(8,128)(2,1)S(1)}, bf16[1024,512]{1,0:T(8,128)(2,1)}, u32[]{:S(2)}) copy-start(bf16[1024,512]{1,0:T(8,128)(2,1)} %w_inner_ref.1) | copy-start | bytes 3145732
  3.3 1.2 %copy-start.1 = (bf16[512,1024]{1,0:T(8,128)(2,1)S(1)}, bf16[512,1024]{1,0:T(8,128)(2,1)}, u32[]{:S(2)}) copy-start(bf16[512,1024]{1,0:T(8,128)(2,1)} %w_outer_ref.1) | copy-start | bytes 3145732
  4.5 1.0 %copy-start.2 = (bf16[1024,256]{1,0:T(8,128)(2,1)S(1)}, bf16[1024,256]{1,0:T(8,128)(2,1)}, u32[]{:S(2)}) copy-start(bf16[1024,256]{1,0:T(8,128)(2,1)} %w_query_ref.1) | copy-start | bytes 1572868
  5.5 1.0 %copy-start.3 = (bf16[1024,256]{1,0:T(8,128)(2,1)S(1)}, bf16[1024,256]{1,0:T(8,128)(2,1)}, u32[]{:S(2)}) copy-start(bf16[1024,256]{1,0:T(8,128)(2,1)} %w_key_ref.1) | copy-start | bytes 1572868
  6.6 1.0 %copy-start.4 = (bf16[1024,256]{1,0:T(8,128)(2,1)S(1)}, bf16[1024,256]{1,0:T(8,128)(2,1)}, u32[]{:S(2)}) copy-start(bf16[1024,256]{1,0:T(8,128)(2,1)} %w_value_ref.1) | copy-start | bytes 1572868
  7.6 1.0 %copy-start.5 = (bf16[256,1024]{1,0:T(8,128)(2,1)S(1)}, bf16[256,1024]{1,0:T(8,128)(2,1)}, u32[]{:S(2)}) copy-start(bf16[256,1024]{1,0:T(8,128)(2,1)} %w_out_ref.1) | copy-start | bytes 1572868
  8.7 0.8 %copy-start.6 = (bf16[128,256]{1,0:T(8,128)(2,1)S(1)}, bf16[128,256]{1,0:T(8,128)(2,1)}, u32[]{:S(2)}) copy-start(bf16[128,256]{1,0:T(8,128)(2,1)} %tokens_ref.1) | copy-start | bytes 196612
  9.5 0.8 %copy-start.7 = (bf16[2,64,256]{2,1,0:T(8,128)(2,1)S(1)}, bf16[2,64,256]{2,1,0:T(8,128)(2,1)}, u32[]{:S(2)}) copy-start(bf16[2,64,256]{2,1,0:T(8,128)(2,1)} %cache_k_ref.1) | copy-start | bytes 196612
  10.3 0.8 %copy-start.8 = (bf16[2,64,256]{2,1,0:T(8,128)(2,1)S(1)}, bf16[2,64,256]{2,1,0:T(8,128)(2,1)}, u32[]{:S(2)}) copy-start(bf16[2,64,256]{2,1,0:T(8,128)(2,1)} %cache_v_ref.1) | copy-start | bytes 196612

commit v2 on v1

--- a/solution.py
+++ b/solution.py
@@ -41,21 +41,27 @@
 
 def kernel(
     tokens_ref,
-    attn_gain_ref,
-    ffn_gain_ref,
+    attn_gain_hbm,
+    ffn_gain_hbm,
     w_query_ref,
     w_key_ref,
     w_value_ref,
     w_out_ref,
     w_inner_ref,
     w_outer_ref,
-    bias_ref,
+    bias_hbm,
     cache_k_ref,
     cache_v_ref,
+    counts_hbm,
+    lengths_hbm,
+    deal_hbm,
+    out_ref,
+    attn_gain_ref,
+    ffn_gain_ref,
+    bias_ref,
     counts_ref,
     lengths_ref,
     deal_ref,
-    out_ref,
     x_full,
     w_qkv,
     w_out,
@@ -94,7 +100,7 @@
     model = w_qkv.shape[0]
     requests, cached, _ = cache_k_ref.shape
     slots = tokens // requests
-    heads = bias_ref.shape[1]
+    heads = bias_ref.shape[0]
     hdim = width // heads
     keys = cached + slots
     own = tokens // TP
@@ -128,6 +134,12 @@
         for i, (src, dst) in enumerate(
             [
                 (tokens_ref, x_full.at[:, own_cols]),
+                (bias_hbm, bias_ref),
+                (counts_hbm, counts_ref),
+                (lengths_hbm, lengths_ref),
+                (deal_hbm, deal_ref),
+                (attn_gain_hbm, attn_gain_ref),
+                (ffn_gain_hbm, ffn_gain_ref),
                 (w_query_ref, w_qkv.at[:, pl.ds(0, width)]),
                 (w_key_ref, w_qkv.at[:, pl.ds(width, width)]),
                 (w_value_ref, w_qkv.at[:, pl.ds(2 * width, width)]),
@@ -158,16 +170,19 @@
         copy.start()
         gathers.append(copy)
 
+    for load in loads[1:7]:
+        load.wait()
+
     key = iota((slots, keys), 1)
     query = iota((slots, keys), 0)
     for r in range(requests):
-        length = lengths_ref[r, 0]
+        length = lengths_ref[r]
         position = jnp.where(key < cached, key, length + key - cached)
         bucket = bucket_of(position - (length + query))
         rows = [jnp.zeros((slots, keys), F32) for _ in range(heads)]
         for b in range(BUCKETS):
             here = bucket == b
-            rows = [jnp.where(here, bias_ref[b, h], rows[h]) for h in range(heads)]
+            rows = [jnp.where(here, bias_ref[h, b], rows[h]) for h in range(heads)]
         for h in range(heads):
             bias[r, pl.ds(h * slots, slots), :] = rows[h]
 
@@ -175,7 +190,7 @@
     k_col = iota((tokens, tokens), 1)
     q_side, q_z = q_row // DEPTH, q_row % DEPTH
     destination = (q_side // 2) * (2 * DEPTH) + q_z * 2 + q_side % 2
-    count_of = jnp.where(k_col // slots == 0, counts_ref[0, 0], counts_ref[requests - 1, 0])
+    count_of = jnp.where(k_col // slots == 0, counts_ref[0], counts_ref[requests - 1])
     live = (k_col % slots) < count_of
     order = jnp.where((deal_ref[...] == destination) & live, 1.0, 0.0)
 
@@ -185,12 +200,12 @@
     stream = x_full[...].astype(F32)
     inverse = lax.rsqrt(jnp.mean(stream * stream, axis=1, keepdims=True) + EPSILON)
     normed = (stream * inverse * attn_gain_ref[...]).astype(BF16)
-    for load in loads[1:4]:
+    for load in loads[7:10]:
         load.wait()
     qkv = dot(normed, w_qkv[...]).astype(BF16)
 
-    loads[4].wait()
-    loads[5].wait()
+    loads[10].wait()
+    loads[11].wait()
     lane_head = iota((slots, width), 1) // hdim
     key_row = iota((heads * slots, keys), 1)
     contexts = []
@@ -203,7 +218,7 @@
             [jnp.where(lane_head == h, queries, jnp.zeros_like(queries)) for h in range(heads)], axis=0
         )
         scores = dot_t(stacked, all_keys) + bias[r]
-        limit = jnp.where(key_row < cached, lengths_ref[r, 0], cached + counts_ref[r, 0])
+        limit = jnp.where(key_row < cached, lengths_ref[r], cached + counts_ref[r])
         scores = jnp.where(key_row < limit, scores, -1e30)
         weights = jnp.exp(scores - jnp.max(scores, axis=1, keepdims=True))
         probs = (weights / jnp.sum(weights, axis=1, keepdims=True)).astype(BF16)
@@ -215,7 +230,7 @@
     context = jnp.concatenate(contexts, axis=0)
 
     moved = dot(order.astype(BF16), context).astype(BF16)
-    loads[6].wait()
+    loads[12].wait()
     partial[...] = dot(moved, w_out[...])
     send_rows[...] = partial[...].astype(BF16)
     row_sends = []
@@ -236,7 +251,7 @@
     own_k = iota((own, tokens), 1)
     own_side, own_z = own_q // DEPTH, own_q % DEPTH
     own_destination = (own_side // 2) * (2 * DEPTH) + own_z * 2 + own_side % 2
-    own_count = jnp.where(own_k // slots == 0, counts_ref[0, 0], counts_ref[requests - 1, 0])
+    own_count = jnp.where(own_k // slots == 0, counts_ref[0], counts_ref[requests - 1])
     own_order = one_hot((deal_ref[...] == own_destination) & ((own_k % slots) < own_count))
     mixed = dot(own_order, x_full[...]) + partial[own_rows, :]
 
@@ -257,8 +272,8 @@
         )
         copy.start()
         ffn_gathers.append(copy)
-    loads[7].wait()
-    loads[8].wait()
+    loads[13].wait()
+    loads[14].wait()
     for copy in ffn_gathers:
         copy.wait_recv()
 
@@ -367,16 +382,19 @@
     own = rows // TP
     hbm = pl.BlockSpec(memory_space=pltpu.HBM)
     vmem = pl.BlockSpec(memory_space=pltpu.VMEM)
-    smem = pl.BlockSpec(memory_space=pltpu.SMEM)
     dma = pltpu.SemaphoreType.DMA
     return pl.pallas_call(
         kernel,
         out_shape=jax.ShapeDtypeStruct((rows, width), BF16),
-        in_specs=[
-            hbm, vmem, vmem, hbm, hbm, hbm, hbm, hbm, hbm, smem, hbm, hbm, smem, smem, vmem,
-        ],
+        in_specs=[hbm] * 15,
         out_specs=vmem,
         scratch_shapes=[
+            pltpu.VMEM((1, model), F32),
+            pltpu.VMEM((1, model), F32),
+            pltpu.SMEM((heads, BUCKETS), F32),
+            pltpu.SMEM((requests,), jnp.int32),
+            pltpu.SMEM((requests,), jnp.int32),
+            pltpu.VMEM((1, rows), jnp.int32),
             pltpu.VMEM((rows, model), BF16),
             pltpu.VMEM((model, 3 * width), BF16),
             pltpu.VMEM((width, model), BF16),
@@ -395,7 +413,7 @@
             pltpu.VMEM((SIDES, DEPTH, width), BF16),
             pltpu.VMEM((DEPTH, 2 * SIDES, width // 2), BF16),
             pltpu.VMEM((DEPTH, 2 * SIDES, width // 2), BF16),
-            dma((9,)),
+            dma((15,)),
             dma((TP - 1,)),
             dma((TP - 1,)),
             dma((TP - 1,)),
@@ -410,7 +428,7 @@
             dma((DEPTH - 1,)),
         ],
         compiler_params=pltpu.CompilerParams(
-            collective_id=0, has_side_effects=True, vmem_limit_bytes=40 * 1024 * 1024
+            collective_id=0, has_side_effects=True, vmem_limit_bytes=60 * 1024 * 1024
         ),
     )(
         tokens,
@@ -422,11 +440,11 @@
         w_out,
         w_inner,
         w_outer,
-        bias_table,
+        bias_table.T,
         cache_keys,
         cache_values,
-        new_counts,
-        cached_lengths,
+        new_counts.reshape(requests),
+        cached_lengths.reshape(requests),
         deal,
     )
 

time: 62 us -> 51.1 us (0.82)
  local copies, waits for them, and re-layouts: 11.8 us -> 1.47 us
    unnamed x34 -> x1, local copies, waits for them, and re-layouts: 11.8 us -> 1.47 us
where the time goes in v2:
time: 51.1 us; the launch traced here: 50.7 us
  Pallas kernels  49.3 us (96%)
  local copies, waits for them, and re-layouts  1.47 us (3%)
    pallas_call x1, Pallas kernels, on_device(): pl.pallas_call(kernel, out_shape=jax.ShapeDtypeStruct((rows, width), BF16...  49.3 us
    unnamed x1, local copies, waits for them, and re-layouts  1.47 us

profile of v2, /device:TPU:1, one launch (start us, length us, event | category | flops | bytes accessed | tf_op | source)
XLA Modules:
  0.0 50.7 jit_solution(9075227018130268529)
XLA Ops:
  0.0 49.3 %shard_map.145 = bf16[128,256]{1,0:T(8,128)(2,1)} custom-call(bf16[128,256]{1,0:T(8,128)(2,1)} %tokens_ref.1, f32[1,1024]{1,0:T(1,128)} %bitcast.5, f32[1,1024]{1,0:T(1,128)} %bitcast.6, bf16[1024,256]{1,0:T(8,128)(2,1)} %w_query_ref.1, bf16[1024,256]{1,0:T(8,128)(2,1)} %w_key_ref.1, bf16[1024,256]{1,0:T(8,128)(2,1)} %w_value_ref.1, ...), custom_call_target="tpu_custom_call" | custom-call | tf_op jit(solution)/shard_map/pallas_call | solution.py:386
  49.3 1.5 %copy.17 = bf16[128,256]{1,0:T(8,128)(2,1)} copy(bf16[128,256]{1,0:T(8,128)(2,1)} %shard_map.145) | data formatting | bytes 131072

commit v3 on v2

--- a/solution.py
+++ b/solution.py
@@ -9,8 +9,12 @@
 THRESHOLDS = (12, 16, 23, 32, 46, 64, 91)
 BUCKETS = 32
 TP = 4
+REPLICAS = 128
 SIDES = 8
 DEPTH = 16
+LANES_OF_ROW = 8
+FAR_FIRST = sorted(range(1, 32), key=lambda slot: -min(2 * slot % DEPTH, -2 * slot % DEPTH))
+NEAR = (1, 2, 14, 15)
 MESH = pl.DeviceIdType.MESH
 BF16 = jnp.bfloat16
 F32 = jnp.float32
@@ -76,10 +80,9 @@
     ffn_full,
     send_cols,
     recv_cols,
-    side_send,
-    side_recv,
-    z_send,
-    z_recv,
+    slab,
+    deal_send,
+    deal_recv,
     load_sem,
     ag_send,
     ag_recv,
@@ -89,10 +92,11 @@
     ag2_recv,
     rs2_send,
     rs2_recv,
-    side_send_sem,
-    side_recv_sem,
-    z_send_sem,
-    z_recv_sem,
+    deal_send_sem,
+    deal_recv_sem,
+    relay_two,
+    relay_four,
+    relay_side,
 ):
     rep = lax.axis_index("rep")
     tp = lax.axis_index("tp")
@@ -112,19 +116,21 @@
 
     def side_peer(offset):
         other = (side + offset) % SIDES
-        return other, (other // 2) * (2 * DEPTH) + z_at * 2 + other % 2
+        return (other // 2) * (2 * DEPTH) + z_at * 2 + other % 2
 
     def z_peer(offset):
-        other = (z_at + offset) % DEPTH
-        return other, x_at * (2 * DEPTH) + other * 2 + core
+        return x_at * (2 * DEPTH) + ((z_at + offset) % DEPTH) * 2 + core
+
+    def greet(semaphore, peer):
+        pl.semaphore_signal(semaphore, inc=1, device_id={"rep": peer}, device_id_type=MESH)
 
     barrier = pltpu.get_barrier_semaphore()
     for offset in range(1, TP):
         pl.semaphore_signal(barrier, inc=1, device_id={"tp": tp_peer(offset)}, device_id_type=MESH)
     for offset in range(1, SIDES):
-        pl.semaphore_signal(barrier, inc=1, device_id={"rep": side_peer(offset)[1]}, device_id_type=MESH)
-    for offset in range(1, DEPTH):
-        pl.semaphore_signal(barrier, inc=1, device_id={"rep": z_peer(offset)[1]}, device_id_type=MESH)
+        greet(barrier, side_peer(offset))
+    for offset in NEAR:
+        greet(barrier, z_peer(offset))
 
     own_cols = pl.ds(pl.multiple_of(tp * width, width), width)
     own_rows = pl.ds(pl.multiple_of(tp * own, own), own)
@@ -154,7 +160,9 @@
     for load in loads:
         load.start()
 
-    pl.semaphore_wait(barrier, (TP - 1) + (SIDES - 1) + (DEPTH - 1))
+    pl.semaphore_wait(barrier, (TP - 1) + (SIDES - 1) + len(NEAR))
+    for offset in (2, DEPTH - 2):
+        greet(relay_two, z_peer(offset))
 
     loads[0].wait()
     gathers = []
@@ -188,11 +196,14 @@
 
     q_row = iota((tokens, tokens), 0)
     k_col = iota((tokens, tokens), 1)
-    q_side, q_z = q_row // DEPTH, q_row % DEPTH
-    destination = (q_side // 2) * (2 * DEPTH) + q_z * 2 + q_side % 2
+    destination = (rep + q_row // own + TP * (q_row % own)) % REPLICAS
     count_of = jnp.where(k_col // slots == 0, counts_ref[0], counts_ref[requests - 1])
     live = (k_col % slots) < count_of
     order = jnp.where((deal_ref[...] == destination) & live, 1.0, 0.0)
+
+    pl.semaphore_wait(relay_two, 2)
+    for offset in (4, DEPTH - 4):
+        greet(relay_four, z_peer(offset))
 
     for copy in gathers:
         copy.wait_recv()
@@ -247,10 +258,13 @@
         copy.start()
         row_sends.append(copy)
 
-    own_q = iota((own, tokens), 0) + tp * own
+    pl.semaphore_wait(relay_four, 2)
+    for offset in range(1, SIDES):
+        greet(relay_side, side_peer(offset))
+
+    own_q = iota((own, tokens), 0)
     own_k = iota((own, tokens), 1)
-    own_side, own_z = own_q // DEPTH, own_q % DEPTH
-    own_destination = (own_side // 2) * (2 * DEPTH) + own_z * 2 + own_side % 2
+    own_destination = (rep + tp + TP * own_q) % REPLICAS
     own_count = jnp.where(own_k // slots == 0, counts_ref[0], counts_ref[requests - 1])
     own_order = one_hot((deal_ref[...] == own_destination) & ((own_k % slots) < own_count))
     mixed = dot(own_order, x_full[...]) + partial[own_rows, :]
@@ -258,6 +272,42 @@
     for copy in row_sends:
         copy.wait_recv()
     mixed = mixed + (recv_rows[0].astype(F32) + recv_rows[1].astype(F32) + recv_rows[2].astype(F32))
+    for c in range(LANES_OF_ROW):
+        slab[pl.ds(c, own, stride=LANES_OF_ROW), :] = mixed[:, c * 128 : (c + 1) * 128]
+    deal_send[...] = slab[...].reshape(own, LANES_OF_ROW, 128).astype(BF16)
+
+    pl.semaphore_wait(relay_side, SIDES - 1)
+
+    def deal(slot):
+        return pltpu.make_async_remote_copy(
+            src_ref=deal_send.at[slot],
+            dst_ref=deal_recv.at[slot],
+            send_sem=deal_send_sem.at[slot],
+            recv_sem=deal_recv_sem.at[slot],
+            device_id={"rep": (rep + tp + TP * slot) % REPLICAS},
+            device_id_type=MESH,
+        )
+
+    for slot in FAR_FIRST:
+        deal(slot).start()
+
+    stays = pltpu.make_async_copy(deal_send.at[0], deal_recv.at[0], deal_recv_sem.at[0])
+
+    @pl.when(tp == 0)
+    def _():
+        stays.start()
+
+    @pl.when(tp != 0)
+    def _():
+        deal(0).start()
+
+    for slot in range(1, own):
+        deal(slot).wait_recv()
+    stays.wait()
+    slab[...] = deal_recv[...].astype(F32).reshape(own * LANES_OF_ROW, 128)
+    mixed = jnp.concatenate(
+        [slab[pl.ds(c, own, stride=LANES_OF_ROW), :] for c in range(LANES_OF_ROW)], axis=1
+    )
     inverse_ffn = lax.rsqrt(jnp.mean(mixed * mixed, axis=1, keepdims=True) + EPSILON)
     ffn_full[own_rows, :] = (mixed * inverse_ffn * ffn_gain_ref[...]).astype(BF16)
     ffn_gathers = []
@@ -294,66 +344,22 @@
         )
         copy.start()
         col_sends.append(copy)
-    to_row = iota((2 * tokens, 2 * tokens), 0)
-    to_col = iota((2 * tokens, 2 * tokens), 1)
-    gather_z = one_hot(
-        to_col
-        == ((to_row // SIDES) % 2) * tokens + (to_row % SIDES) * DEPTH + to_row // (2 * SIDES)
-    )
+    from_row = iota((tokens, tokens), 1)
+    source = (rep + REPLICAS * 2 - from_row // own - TP * (from_row % own)) % REPLICAS
+    restore = one_hot(iota((tokens, tokens), 0) == source)
     final = partial[:, own_cols]
     for copy in col_sends:
         copy.wait_recv()
     final = final + (recv_cols[0].astype(F32) + recv_cols[1].astype(F32) + recv_cols[2].astype(F32))
-    side_send[...] = final.astype(BF16).reshape(SIDES, DEPTH, width)
-
-    side_sends = []
-    for offset in range(1, SIDES):
-        other, peer = side_peer(offset)
-        copy = pltpu.make_async_remote_copy(
-            src_ref=side_send.at[other],
-            dst_ref=side_recv.at[side],
-            send_sem=side_send_sem.at[offset - 1],
-            recv_sem=side_recv_sem.at[offset - 1],
-            device_id={"rep": peer},
-            device_id_type=MESH,
-        )
-        copy.start()
-        side_sends.append(copy)
-    side_recv[side] = side_send[side]
-    d_row = iota((tokens, 2 * tokens), 0)
-    d_col = iota((tokens, 2 * tokens), 1)
-    d_from = ((d_row // 2) % DEPTH) * (2 * SIDES) + (d_row // (2 * DEPTH)) * 2 + d_row % 2
-    left = one_hot(d_col == d_from)
-    right = one_hot(d_col == d_from + SIDES)
-    for copy in side_sends:
-        copy.wait_recv()
-
-    arrived = side_recv[...].reshape(tokens, width)
-    halves = jnp.concatenate([arrived[:, : width // 2], arrived[:, width // 2 :]], axis=0)
-    z_send[...] = dot(gather_z, halves).astype(BF16).reshape(DEPTH, 2 * SIDES, width // 2)
-    z_sends = []
-    for offset in range(1, DEPTH):
-        other, peer = z_peer(offset)
-        copy = pltpu.make_async_remote_copy(
-            src_ref=z_send.at[other],
-            dst_ref=z_recv.at[z_at],
-            send_sem=z_send_sem.at[offset - 1],
-            recv_sem=z_recv_sem.at[offset - 1],
-            device_id={"rep": peer},
-            device_id_type=MESH,
-        )
-        copy.start()
-        z_sends.append(copy)
-    z_recv[z_at] = z_send[z_at]
-    for copy in gathers + row_sends + ffn_gathers + col_sends + side_sends:
+    out_ref[...] = dot(restore, final.astype(BF16)).astype(BF16)
+    for copy in gathers + row_sends + ffn_gathers + col_sends:
         copy.wait_send()
-    for copy in z_sends:
-        copy.wait_recv()
-    landed = z_recv[...].reshape(2 * tokens, width // 2)
-    out_ref[:, : width // 2] = dot(left, landed).astype(BF16)
-    out_ref[:, width // 2 :] = dot(right, landed).astype(BF16)
-    for copy in z_sends:
-        copy.wait_send()
+    for slot in range(1, own):
+        deal(slot).wait_send()
+
+    @pl.when(tp != 0)
+    def _():
+        deal(0).wait_send()
 
 
 def on_device(
@@ -409,10 +415,9 @@
             pltpu.VMEM((rows, model), BF16),
             pltpu.VMEM((rows, model), BF16),
             pltpu.VMEM((TP - 1, rows, width), BF16),
-            pltpu.VMEM((SIDES, DEPTH, width), BF16),
-            pltpu.VMEM((SIDES, DEPTH, width), BF16),
-            pltpu.VMEM((DEPTH, 2 * SIDES, width // 2), BF16),
-            pltpu.VMEM((DEPTH, 2 * SIDES, width // 2), BF16),
+            pltpu.VMEM((own * LANES_OF_ROW, 128), F32),
+            pltpu.VMEM((own, LANES_OF_ROW, 128), BF16),
+            pltpu.VMEM((own, LANES_OF_ROW, 128), BF16),
             dma((15,)),
             dma((TP - 1,)),
             dma((TP - 1,)),
@@ -422,10 +427,11 @@
             dma((TP - 1,)),
             dma((TP - 1,)),
             dma((TP - 1,)),
-            dma((SIDES - 1,)),
-            dma((SIDES - 1,)),
-            dma((DEPTH - 1,)),
-            dma((DEPTH - 1,)),
+            dma((own,)),
+            dma((own,)),
+            pltpu.SemaphoreType.REGULAR,
+            pltpu.SemaphoreType.REGULAR,
+            pltpu.SemaphoreType.REGULAR,
         ],
         compiler_params=pltpu.CompilerParams(
             collective_id=0, has_side_effects=True, vmem_limit_bytes=60 * 1024 * 1024

time: 51.1 us -> 46.1 us (0.902)
  Pallas kernels: 49.3 us -> 44.5 us
    pallas_call x1, Pallas kernels: 49.3 us -> 44.5 us  [on_device(): pl.pallas_call(kernel, out_shape=jax.ShapeDtypeStruct((rows, width), BF16...]
where the time goes in v3:
time: 46.1 us; the launch traced here: 46 us
  Pallas kernels  44.5 us (97%)
  local copies, waits for them, and re-layouts  1.47 us (3%)
    pallas_call x1, Pallas kernels, on_device(): pl.pallas_call(kernel, out_shape=jax.ShapeDtypeStruct((rows, width), BF16...  44.5 us
    unnamed x1, local copies, waits for them, and re-layouts  1.47 us

profile of v3, /device:TPU:1, one launch (start us, length us, event | category | flops | bytes accessed | tf_op | source)
XLA Modules:
  0.0 46.0 jit_solution(7784324712607038838)
XLA Ops:
  0.0 44.5 %shard_map.145 = bf16[128,256]{1,0:T(8,128)(2,1)} custom-call(bf16[128,256]{1,0:T(8,128)(2,1)} %tokens_ref.1, f32[1,1024]{1,0:T(1,128)} %bitcast.5, f32[1,1024]{1,0:T(1,128)} %bitcast.6, bf16[1024,256]{1,0:T(8,128)(2,1)} %w_query_ref.1, bf16[1024,256]{1,0:T(8,128)(2,1)} %w_key_ref.1, bf16[1024,256]{1,0:T(8,128)(2,1)} %w_value_ref.1, ...), custom_call_target="tpu_custom_call" | custom-call | tf_op jit(solution)/shard_map/pallas_call | solution.py:392
  44.5 1.5 %copy.17 = bf16[128,256]{1,0:T(8,128)(2,1)} copy(bf16[128,256]{1,0:T(8,128)(2,1)} %shard_map.145) | data formatting | bytes 131072

commit v4 on v3

--- a/solution.py
+++ b/solution.py
@@ -13,7 +13,7 @@
 SIDES = 8
 DEPTH = 16
 LANES_OF_ROW = 8
-FAR_FIRST = sorted(range(1, 32), key=lambda slot: -min(2 * slot % DEPTH, -2 * slot % DEPTH))
+HALF = 16
 NEAR = (1, 2, 14, 15)
 MESH = pl.DeviceIdType.MESH
 BF16 = jnp.bfloat16
@@ -37,6 +37,17 @@
     larger = 8 + sum(((distance >= threshold).astype(jnp.int32) for threshold in THRESHOLDS))
     near = jnp.where(distance < 8, distance, larger)
     return near + 16 * (relative > 0).astype(jnp.int32)
+
+
+def step_of(slot):
+    return ((slot % HALF) // 4) * 8 + (slot % 4 + 6 + 4 * (slot // HALF)) % 8
+
+
+STAYS = 2
+
+
+def far_first(slots):
+    return sorted(slots, key=lambda slot: -min(2 * step_of(slot) % DEPTH, -2 * step_of(slot) % DEPTH))
 
 
 def one_hot(condition):
@@ -80,6 +91,7 @@
     ffn_full,
     send_cols,
     recv_cols,
+    mixed_ref,
     slab,
     deal_send,
     deal_recv,
@@ -133,7 +145,10 @@
         greet(barrier, z_peer(offset))
 
     own_cols = pl.ds(pl.multiple_of(tp * width, width), width)
-    own_rows = pl.ds(pl.multiple_of(tp * own, own), own)
+
+    def group_rows(half, group):
+        return pl.ds(pl.multiple_of((half * TP + group) * HALF, HALF), HALF)
+
 
     loads = [
         pltpu.make_async_copy(src, dst, load_sem.at[i])
@@ -181,6 +196,13 @@
     for load in loads[1:7]:
         load.wait()
 
+    def squares_of(chunk):
+        cols = pl.ds(pl.multiple_of(chunk * width, width), width)
+        stream = x_full[:, cols].astype(F32)
+        return jnp.sum(stream * stream, axis=1, keepdims=True)
+
+    squares = squares_of(tp)
+
     key = iota((slots, keys), 1)
     query = iota((slots, keys), 0)
     for r in range(requests):
@@ -196,7 +218,9 @@
 
     q_row = iota((tokens, tokens), 0)
     k_col = iota((tokens, tokens), 1)
-    destination = (rep + q_row // own + TP * (q_row % own)) % REPLICAS
+    q_group = (q_row // HALF) % TP
+    q_step = step_of(q_row // (TP * HALF) * HALF + q_row % HALF)
+    destination = (rep + q_group + TP * q_step) % REPLICAS
     count_of = jnp.where(k_col // slots == 0, counts_ref[0], counts_ref[requests - 1])
     live = (k_col % slots) < count_of
     order = jnp.where((deal_ref[...] == destination) & live, 1.0, 0.0)
@@ -205,15 +229,16 @@
     for offset in (4, DEPTH - 4):
         greet(relay_four, z_peer(offset))
 
-    for copy in gathers:
-        copy.wait_recv()
-
-    stream = x_full[...].astype(F32)
-    inverse = lax.rsqrt(jnp.mean(stream * stream, axis=1, keepdims=True) + EPSILON)
-    normed = (stream * inverse * attn_gain_ref[...]).astype(BF16)
     for load in loads[7:10]:
         load.wait()
-    qkv = dot(normed, w_qkv[...]).astype(BF16)
+    for copy, offset in ((gathers[1], 1), (gathers[2], 3), (gathers[0], 2)):
+        copy.wait_recv()
+        squares += squares_of((tp + TP - offset) % TP)
+    inverse = lax.rsqrt(squares / model + EPSILON)
+    for c in range(TP):
+        cols = slice(c * width, (c + 1) * width)
+        send_rows[:, cols] = (x_full[:, cols].astype(F32) * inverse * attn_gain_ref[:, cols]).astype(BF16)
+    qkv = dot(send_rows[...], w_qkv[...]).astype(BF16)
 
     loads[10].wait()
     loads[11].wait()
@@ -244,19 +269,20 @@
     loads[12].wait()
     partial[...] = dot(moved, w_out[...])
     send_rows[...] = partial[...].astype(BF16)
-    row_sends = []
-    for offset in (2, 1, 3):
-        peer = tp_peer(offset)
-        copy = pltpu.make_async_remote_copy(
-            src_ref=send_rows.at[pl.ds(pl.multiple_of(peer * own, own), own), :],
-            dst_ref=recv_rows.at[offset - 1],
-            send_sem=rs_send.at[offset - 1],
-            recv_sem=rs_recv.at[offset - 1],
-            device_id={"tp": peer},
-            device_id_type=MESH,
-        )
-        copy.start()
-        row_sends.append(copy)
+    row_sends = [[], []]
+    for half in (1, 0):
+        for offset in (2, 1, 3):
+            peer = tp_peer(offset)
+            copy = pltpu.make_async_remote_copy(
+                src_ref=send_rows.at[group_rows(half, peer), :],
+                dst_ref=recv_rows.at[half, offset - 1],
+                send_sem=rs_send.at[half, offset - 1],
+                recv_sem=rs_recv.at[half, offset - 1],
+                device_id={"tp": peer},
+                device_id_type=MESH,
+            )
+            copy.start()
+            row_sends[half].append(copy)
 
     pl.semaphore_wait(relay_four, 2)
     for offset in range(1, SIDES):
@@ -264,19 +290,10 @@
 
     own_q = iota((own, tokens), 0)
     own_k = iota((own, tokens), 1)
-    own_destination = (rep + tp + TP * own_q) % REPLICAS
+    own_destination = (rep + tp + TP * step_of(own_q)) % REPLICAS
     own_count = jnp.where(own_k // slots == 0, counts_ref[0], counts_ref[requests - 1])
     own_order = one_hot((deal_ref[...] == own_destination) & ((own_k % slots) < own_count))
-    mixed = dot(own_order, x_full[...]) + partial[own_rows, :]
-
-    for copy in row_sends:
-        copy.wait_recv()
-    mixed = mixed + (recv_rows[0].astype(F32) + recv_rows[1].astype(F32) + recv_rows[2].astype(F32))
-    for c in range(LANES_OF_ROW):
-        slab[pl.ds(c, own, stride=LANES_OF_ROW), :] = mixed[:, c * 128 : (c + 1) * 128]
-    deal_send[...] = slab[...].reshape(own, LANES_OF_ROW, 128).astype(BF16)
-
-    pl.semaphore_wait(relay_side, SIDES - 1)
+    mixed_ref[...] = dot(own_order, x_full[...])
 
     def deal(slot):
         return pltpu.make_async_remote_copy(
@@ -284,14 +301,28 @@
             dst_ref=deal_recv.at[slot],
             send_sem=deal_send_sem.at[slot],
             recv_sem=deal_recv_sem.at[slot],
-            device_id={"rep": (rep + tp + TP * slot) % REPLICAS},
+            device_id={"rep": (rep + tp + TP * step_of(slot)) % REPLICAS},
             device_id_type=MESH,
         )
 
-    for slot in FAR_FIRST:
-        deal(slot).start()
-
-    stays = pltpu.make_async_copy(deal_send.at[0], deal_recv.at[0], deal_recv_sem.at[0])
+    stays = pltpu.make_async_copy(deal_send.at[STAYS], deal_recv.at[STAYS], deal_recv_sem.at[STAYS])
+    lines = HALF * LANES_OF_ROW
+    for half in (1, 0):
+        for copy in row_sends[half]:
+            copy.wait_recv()
+        rows = slice(half * HALF, (half + 1) * HALF)
+        arrived = [recv_rows[half, i].astype(F32) for i in range(TP - 1)]
+        mixed = mixed_ref[rows, :] + partial[group_rows(half, tp), :] + (arrived[0] + arrived[1] + arrived[2])
+        for c in range(LANES_OF_ROW):
+            slab[pl.ds(half * lines + c, HALF, stride=LANES_OF_ROW), :] = mixed[:, c * 128 : (c + 1) * 128]
+        deal_send[rows] = (
+            slab[half * lines : (half + 1) * lines, :].reshape(HALF, LANES_OF_ROW, 128).astype(BF16)
+        )
+        if half == 1:
+            pl.semaphore_wait(relay_side, SIDES - 1)
+        for slot in far_first(range(half * HALF, (half + 1) * HALF)):
+            if slot != STAYS:
+                deal(slot).start()
 
     @pl.when(tp == 0)
     def _():
@@ -299,67 +330,94 @@
 
     @pl.when(tp != 0)
     def _():
-        deal(0).start()
-
-    for slot in range(1, own):
-        deal(slot).wait_recv()
-    stays.wait()
-    slab[...] = deal_recv[...].astype(F32).reshape(own * LANES_OF_ROW, 128)
-    mixed = jnp.concatenate(
-        [slab[pl.ds(c, own, stride=LANES_OF_ROW), :] for c in range(LANES_OF_ROW)], axis=1
-    )
-    inverse_ffn = lax.rsqrt(jnp.mean(mixed * mixed, axis=1, keepdims=True) + EPSILON)
-    ffn_full[own_rows, :] = (mixed * inverse_ffn * ffn_gain_ref[...]).astype(BF16)
-    ffn_gathers = []
-    for offset in (2, 1, 3):
-        copy = pltpu.make_async_remote_copy(
-            src_ref=ffn_full.at[own_rows, :],
-            dst_ref=ffn_full.at[own_rows, :],
-            send_sem=ag2_send.at[offset - 1],
-            recv_sem=ag2_recv.at[offset - 1],
-            device_id={"tp": tp_peer(offset)},
-            device_id_type=MESH,
+        deal(STAYS).start()
+
+    ffn_gathers = [[], []]
+    for half in (0, 1):
+        rows = slice(half * HALF, (half + 1) * HALF)
+        for slot in range(half * HALF, (half + 1) * HALF):
+            if slot == STAYS:
+                stays.wait()
+            else:
+                deal(slot).wait_recv()
+        slab[half * lines : (half + 1) * lines, :] = deal_recv[rows].astype(F32).reshape(lines, 128)
+        mixed = jnp.concatenate(
+            [
+                slab[pl.ds(half * lines + c, HALF, stride=LANES_OF_ROW), :]
+                for c in range(LANES_OF_ROW)
+            ],
+            axis=1,
         )
-        copy.start()
-        ffn_gathers.append(copy)
+        mixed_ref[rows, :] = mixed
+        inverse_ffn = lax.rsqrt(jnp.mean(mixed * mixed, axis=1, keepdims=True) + EPSILON)
+        ffn_full[group_rows(half, tp), :] = (mixed * inverse_ffn * ffn_gain_ref[...]).astype(BF16)
+        for offset in (2, 1, 3):
+            copy = pltpu.make_async_remote_copy(
+                src_ref=ffn_full.at[group_rows(half, tp), :],
+                dst_ref=ffn_full.at[group_rows(half, tp), :],
+                send_sem=ag2_send.at[half, offset - 1],
+                recv_sem=ag2_recv.at[half, offset - 1],
+                device_id={"tp": tp_peer(offset)},
+                device_id_type=MESH,
+            )
+            copy.start()
+            ffn_gathers[half].append(copy)
+
     loads[13].wait()
     loads[14].wait()
-    for copy in ffn_gathers:
-        copy.wait_recv()
-
-    hidden = jnp.maximum(dot(ffn_full[...], w_inner[...]), 0.0).astype(BF16)
-    partial[...] = dot(hidden, w_outer[...])
-    partial[own_rows, :] = partial[own_rows, :] + mixed
-    send_cols[...] = partial[...].astype(BF16)
-    col_sends = []
-    for offset in (2, 1, 3):
-        peer = tp_peer(offset)
-        copy = pltpu.make_async_remote_copy(
-            src_ref=send_cols.at[:, pl.ds(pl.multiple_of(peer * width, width), width)],
-            dst_ref=recv_cols.at[offset - 1],
-            send_sem=rs2_send.at[offset - 1],
-            recv_sem=rs2_recv.at[offset - 1],
-            device_id={"tp": peer},
-            device_id_type=MESH,
-        )
-        copy.start()
-        col_sends.append(copy)
+    col_sends = [[], []]
+    for half in (0, 1):
+        for copy in ffn_gathers[half]:
+            copy.wait_recv()
+        block = slice(half * TP * HALF, (half + 1) * TP * HALF)
+        hidden = jnp.maximum(dot(ffn_full[block, :], w_inner[...]), 0.0).astype(BF16)
+
+        def project(peer):
+            cols = pl.ds(pl.multiple_of(peer * width, width), width)
+            partial[block, cols] = dot(hidden, w_outer[:, cols])
+            partial[group_rows(half, tp), cols] += mixed_ref[half * HALF : (half + 1) * HALF, cols]
+            return cols
+
+        for offset in (2, 1, 3):
+            peer = tp_peer(offset)
+            cols = project(peer)
+            send_cols[block, cols] = partial[block, cols].astype(BF16)
+            copy = pltpu.make_async_remote_copy(
+                src_ref=send_cols.at[block, cols],
+                dst_ref=recv_cols.at[offset - 1, block, :],
+                send_sem=rs2_send.at[half, offset - 1],
+                recv_sem=rs2_recv.at[half, offset - 1],
+                device_id={"tp": peer},
+                device_id_type=MESH,
+            )
+            copy.start()
+            col_sends[half].append(copy)
+        project(tp)
     from_row = iota((tokens, tokens), 1)
-    source = (rep + REPLICAS * 2 - from_row // own - TP * (from_row % own)) % REPLICAS
+    from_step = step_of(from_row // (TP * HALF) * HALF + from_row % HALF)
+    source = (rep + REPLICAS * 2 - (from_row // HALF) % TP - TP * from_step) % REPLICAS
     restore = one_hot(iota((tokens, tokens), 0) == source)
-    final = partial[:, own_cols]
-    for copy in col_sends:
-        copy.wait_recv()
-    final = final + (recv_cols[0].astype(F32) + recv_cols[1].astype(F32) + recv_cols[2].astype(F32))
-    out_ref[...] = dot(restore, final.astype(BF16)).astype(BF16)
-    for copy in gathers + row_sends + ffn_gathers + col_sends:
+    for copy in gathers + row_sends[0] + row_sends[1] + ffn_gathers[0] + ffn_gathers[1] + col_sends[0]:
         copy.wait_send()
-    for slot in range(1, own):
-        deal(slot).wait_send()
+    for slot in range(own):
+        if slot != STAYS:
+            deal(slot).wait_send()
 
     @pl.when(tp != 0)
     def _():
-        deal(0).wait_send()
+        deal(STAYS).wait_send()
+
+    placed = jnp.zeros((tokens, width), F32)
+    for half in (0, 1):
+        block = slice(half * TP * HALF, (half + 1) * TP * HALF)
+        for copy in col_sends[half]:
+            copy.wait_recv()
+        arrived = [recv_cols[i, block, :].astype(F32) for i in range(TP - 1)]
+        final = partial[block, own_cols] + (arrived[0] + arrived[1] + arrived[2])
+        placed += dot(restore[:, block], final.astype(BF16))
+    out_ref[...] = placed.astype(BF16)
+    for copy in col_sends[1]:
+        copy.wait_send()
 
 
 def on_device(
@@ -411,22 +469,23 @@
             pltpu.VMEM((requests, heads * slots, cached + slots), F32),
             pltpu.VMEM((rows, model), F32),
             pltpu.VMEM((rows, model), BF16),
-            pltpu.VMEM((TP - 1, own, model), BF16),
+            pltpu.VMEM((2, TP - 1, HALF, model), BF16),
             pltpu.VMEM((rows, model), BF16),
             pltpu.VMEM((rows, model), BF16),
             pltpu.VMEM((TP - 1, rows, width), BF16),
+            pltpu.VMEM((own, model), F32),
             pltpu.VMEM((own * LANES_OF_ROW, 128), F32),
             pltpu.VMEM((own, LANES_OF_ROW, 128), BF16),
             pltpu.VMEM((own, LANES_OF_ROW, 128), BF16),
             dma((15,)),
             dma((TP - 1,)),
             dma((TP - 1,)),
-            dma((TP - 1,)),
-            dma((TP - 1,)),
-            dma((TP - 1,)),
-            dma((TP - 1,)),
-            dma((TP - 1,)),
-            dma((TP - 1,)),
+            dma((2, TP - 1)),
+            dma((2, TP - 1)),
+            dma((2, TP - 1)),
+            dma((2, TP - 1)),
+            dma((2, TP - 1)),
+            dma((2, TP - 1)),
             dma((own,)),
             dma((own,)),
             pltpu.SemaphoreType.REGULAR,
@@ -434,9 +493,9 @@
             pltpu.SemaphoreType.REGULAR,
         ],
         compiler_params=pltpu.CompilerParams(
-            collective_id=0, has_side_effects=True, vmem_limit_bytes=60 * 1024 * 1024
+            collective_id=0, has_side_effects=True, vmem_limit_bytes=40 * 1024 * 1024
         ),
-    )(
+    )(*[pltpu.with_memory_space_constraint(a, pltpu.HBM) for a in (
         tokens,
         attn_gain.reshape(1, model),
         ffn_gain.reshape(1, model),
@@ -452,7 +511,7 @@
         new_counts.reshape(requests),
         cached_lengths.reshape(requests),
         deal,
-    )
+    )])
 
 
 def solution(mesh):

time: 46.1 us -> 42.1 us (0.913)
  Pallas kernels: 44.5 us -> 41 us
  local copies, waits for them, and re-layouts: 1.47 us -> 0.63 us
    pallas_call x1, Pallas kernels: 44.5 us -> 41 us  [on_device(): pl.pallas_call(kernel, out_shape=jax.ShapeDtypeStruct((rows, width), BF16...]
    unnamed x1, local copies, waits for them, and re-layouts: 1.47 us -> 0.63 us
where the time goes in v4:
time: 42.1 us; the launch traced here: 41.7 us
  Pallas kernels  41 us (97%)
  local copies, waits for them, and re-layouts  0.63 us (1%)
    pallas_call x1, Pallas kernels, on_device(): pl.pallas_call(kernel, out_shape=jax.ShapeDtypeStruct((rows, width), BF16...  41 us

profile of v4, /device:TPU:1, one launch (start us, length us, event | category | flops | bytes accessed | tf_op | source)
XLA Modules:
  0.0 41.7 jit_solution(17094361758846020156)
XLA Ops:
  0.0 41.0 %shard_map.145 = bf16[128,256]{1,0:T(8,128)(2,1)S(1)} custom-call(bf16[128,256]{1,0:T(8,128)(2,1)} %tokens_ref.1, f32[1,1024]{1,0:T(1,128)} %bitcast.5, f32[1,1024]{1,0:T(1,128)} %bitcast.6, bf16[1024,256]{1,0:T(8,128)(2,1)} %w_query_ref.1, bf16[1024,256]{1,0:T(8,128)(2,1)} %w_key_ref.1, bf16[1024,256]{1,0:T(8,128)(2,1)} %w_value_ref.1, ...), custom_call_target="tpu_custom_call" | custom-call | tf_op jit(solution)/shard_map/pallas_call | solution.py:450
  41.1 0.6 %copy.17 = bf16[128,256]{1,0:T(8,128)(2,1)} copy(bf16[128,256]{1,0:T(8,128)(2,1)S(1)} %shard_map.145) | data formatting | bytes 131072

commit v5 on v4

--- a/solution.py
+++ b/solution.py
@@ -474,7 +474,7 @@
             pltpu.VMEM((rows, model), BF16),
             pltpu.VMEM((TP - 1, rows, width), BF16),
             pltpu.VMEM((own, model), F32),
-            pltpu.VMEM((own * LANES_OF_ROW, 128), F32),
+            pltpu.VMEM((own * LANES_OF_ROW + 8, 128), F32),
             pltpu.VMEM((own, LANES_OF_ROW, 128), BF16),
             pltpu.VMEM((own, LANES_OF_ROW, 128), BF16),
             dma((15,)),

time: 42.1 us -> 42.4 us (level)
  no operation moved by 1% of the time
where the time goes in v5:
time: 42.4 us; the launch traced here: 41.7 us
  Pallas kernels  41 us (97%)
  local copies, waits for them, and re-layouts  0.63 us (1%)
    pallas_call x1, Pallas kernels, on_device(): pl.pallas_call(kernel, out_shape=jax.ShapeDtypeStruct((rows, width), BF16...  41 us

profile of v5, /device:TPU:1, one launch (start us, length us, event | category | flops | bytes accessed | tf_op | source)
XLA Modules:
  0.0 41.7 jit_solution(15366304583270123766)
XLA Ops:
  0.0 41.0 %shard_map.145 = bf16[128,256]{1,0:T(8,128)(2,1)S(1)} custom-call(bf16[128,256]{1,0:T(8,128)(2,1)} %tokens_ref.1, f32[1,1024]{1,0:T(1,128)} %bitcast.5, f32[1,1024]{1,0:T(1,128)} %bitcast.6, bf16[1024,256]{1,0:T(8,128)(2,1)} %w_query_ref.1, bf16[1024,256]{1,0:T(8,128)(2,1)} %w_key_ref.1, bf16[1024,256]{1,0:T(8,128)(2,1)} %w_value_ref.1, ...), custom_call_target="tpu_custom_call" | custom-call | tf_op jit(solution)/shard_map/pallas_call | solution.py:450
  41.1 0.6 %copy.17 = bf16[128,256]{1,0:T(8,128)(2,1)} copy(bf16[128,256]{1,0:T(8,128)(2,1)S(1)} %shard_map.145) | data formatting | bytes 131072

commit v6 on v4

--- a/solution.py
+++ b/solution.py
@@ -267,10 +267,11 @@
 
     moved = dot(order.astype(BF16), context).astype(BF16)
     loads[12].wait()
-    partial[...] = dot(moved, w_out[...])
-    send_rows[...] = partial[...].astype(BF16)
     row_sends = [[], []]
     for half in (1, 0):
+        block = slice(half * TP * HALF, (half + 1) * TP * HALF)
+        partial[block, :] = dot(moved[block], w_out[...])
+        send_rows[block, :] = partial[block, :].astype(BF16)
         for offset in (2, 1, 3):
             peer = tp_peer(offset)
             copy = pltpu.make_async_remote_copy(

time: 42.1 us -> 42 us (level)
  no operation moved by 1% of the time
where the time goes in v6:
time: 42 us; the launch traced here: 41.7 us
  Pallas kernels  41 us (98%)
  local copies, waits for them, and re-layouts  0.63 us (2%)
    pallas_call x1, Pallas kernels, on_device(): pl.pallas_call(kernel, out_shape=jax.ShapeDtypeStruct((rows, width), BF16...  41 us

profile of v6, /device:TPU:1, one launch (start us, length us, event | category | flops | bytes accessed | tf_op | source)
XLA Modules:
  0.0 41.7 jit_solution(9657194833815235363)
XLA Ops:
  0.0 41.0 %shard_map.145 = bf16[128,256]{1,0:T(8,128)(2,1)S(1)} custom-call(bf16[128,256]{1,0:T(8,128)(2,1)} %tokens_ref.1, f32[1,1024]{1,0:T(1,128)} %bitcast.5, f32[1,1024]{1,0:T(1,128)} %bitcast.6, bf16[1024,256]{1,0:T(8,128)(2,1)} %w_query_ref.1, bf16[1024,256]{1,0:T(8,128)(2,1)} %w_key_ref.1, bf16[1024,256]{1,0:T(8,128)(2,1)} %w_value_ref.1, ...), custom_call_target="tpu_custom_call" | custom-call | tf_op jit(solution)/shard_map/pallas_call | solution.py:451
  41.0 0.6 %copy.17 = bf16[128,256]{1,0:T(8,128)(2,1)} copy(bf16[128,256]{1,0:T(8,128)(2,1)S(1)} %shard_map.145) | data formatting | bytes 131072
